TPU v7x, 32 devices: a whole 2x2x4 slice. The times are simulated.
32 devices in a mesh: row: 8 (over z, y), col: 2 (over x), fiber: 2 (over core).
Axes of the slice: x: 2, y: 2, z: 4, core: 2. Of those that a mesh axis runs over, the one named last changes fastest.
Arguments:
- a_panels: float32 [3072, 2, 2, 768], P(('row', 'col'), 'fiber'), may hold values from -12 to 12
- b_panels: float32 [2, 2, 768, 2048], P('fiber', None, 'row', 'col'), may hold values from -0.15625 to 0.15625
- a_pattern: int32 [24, 2, 2, 6], P('row', 'fiber'), may hold values 0 or 1
- c_pattern: int32 [24, 16], P('row', 'col'), may hold values 0 or 1
Outputs:
- scaled: float32 [3072, 2048], P(('row', 'fiber'), 'col')
All inputs are finite; a program needn't handle non-finite values. No bound on the sum of `a_pattern` or of `c_pattern` on one device may be relied on, other than what follows from the above.
Results may differ from a plain program's by a relative error of at most 0.00013.
Values sent between devices are 32-bit elements; how exact they have to be, the bound alone decides.
No kernel may reach another device: no remote copies, remote signals or barrier semaphores. Data moves between devices by JAX's collectives and lax.ppermute only.
A program may use at most 64 MiB of HBM per device.

v0:
```python
import jax
import jax.numpy as jnp
from jax import lax
from jax.sharding import PartitionSpec as P

BLK = 128
EPS = 1e-06


def local(a_panels, b_panels, a_pattern, c_pattern):
    block_size = BLK
    section_count = a_panels.shape[2]
    panel_width = a_panels.shape[3]
    block_rows = a_pattern.shape[0]
    width_blocks = a_pattern.shape[3]
    local_rows = block_rows * block_size
    column_count = b_panels.shape[3]
    running_sum = jnp.zeros((local_rows, column_count), jnp.float32)
    for section_index in range(section_count):
        row_block = lax.all_gather(a_panels[:, 0, section_index, :], "col", axis=0, tiled=True)
        keep_left = a_pattern[:, 0, section_index, :].astype(jnp.float32)
        left_panel = (
            row_block.reshape(block_rows, block_size, width_blocks, block_size)
            * keep_left[:, None, :, None]
        ).reshape(local_rows, panel_width)
        right_panel = lax.all_gather(b_panels[0, section_index], "row", axis=0, tiled=True)
        running_sum = running_sum + jnp.dot(
            left_panel,
            right_panel,
            precision=lax.Precision.HIGHEST,
            preferred_element_type=jnp.float32,
        )
    layer_index = lax.axis_index("fiber")
    fibers = lax.axis_size("fiber")
    share_rows = local_rows // fibers
    keep_product = c_pattern.astype(jnp.float32)
    keep_full = jnp.broadcast_to(
        keep_product[:, None, :, None], (block_rows, block_size, keep_product.shape[1], block_size)
    ).reshape(local_rows, column_count)
    merged = lax.psum_scatter(running_sum, "fiber", scatter_dimension=0, tiled=True)
    keep_share = lax.dynamic_slice_in_dim(keep_full, layer_index * share_rows, share_rows, 0)
    product = merged * keep_share
    inflated = product * product
    totals = lax.psum(jnp.sum(inflated, axis=0), ("row", "fiber"))
    row_count = share_rows * lax.axis_size("row") * fibers
    return inflated / (totals / row_count + EPS)


def solution(mesh):
    placed = (
        P(("row", "col"), "fiber", None, None),
        P("fiber", None, "row", "col"),
        P("row", "fiber", None, None),
        P("row", "col"),
    )
    return jax.shard_map(
        local, mesh=mesh, in_specs=placed, out_specs=P(("row", "fiber"), "col"), check_vma=False
    )
```

profile of v0, /device:TPU:0, one launch (start us, length us, event | category | flops | bytes accessed | tf_op | source)
XLA Modules:
  0.0 241.1 jit_solution(13269795928993399024)
XLA Ops:
  6.5 0.0 all-gather.13.cloned.1.call-start
  6.5 2.8 %fusion.12 = (f32[192,1,1,768]{3,2,1,0:T(1,128)S(1)}, f32[192,1,1,768]{3,2,1,0:T(1,128)S(1)}) fusion(f32[192,1,2,768]{3,2,1,0:T(2,128)} %param.4), kind=kLoop, calls=%fused_computation.20 | loop fusion | bytes 2359296 | tf_op jit(solution)/shard_map/slice | solution.py:20
  9.3 0.9 copy.10
  10.2 0.0 all-gather.13.cloned.1.call-update
  10.2 0.0 all-gather.15.cloned.1.call-start
  10.2 0.0 copy-done.3
  10.2 0.9 fusion.13
  11.2 0.0 all-gather.15.cloned.1.call-update
  11.2 0.0 all-gather.9.cloned.1.call-start
  11.3 0.9 copy.9
  12.2 0.0 all-gather.9.cloned.1.call-update
  12.2 0.0 all-gather.11.cloned.1.call-start
  12.3 0.5 all-gather.11.cloned.1.call-update
  12.8 0.0 reduce-scatter.2.cloned.1.call-start
  12.8 0.0 copy-done.4
  12.9 23.0 %all-gather.13.cloned.1.call-done = f32[384,1,1,768]{3,0,2,1:T(8,128)} async-done(((f32[192,1,1,768]{3,0,2,1:T(8,128)}), f32[384,1,1,768]{3,0,2,1:T(8,128)}) %all-gather.13.cloned.1.call-update) | async-done | bytes 1179664 | tf_op jit(solution)/shard_map/all_gather | solution.py:20
  35.8 62.2 %all-gather.15.cloned.1.call-done = f32[1,1,768,1024]{3,2,1,0:T(8,128)} async-done(((f32[1,1,96,1024]{3,2,1,0:T(8,128)}), f32[1,1,768,1024]{3,2,1,0:T(8,128)}) %all-gather.15.cloned.1.call-update) | async-done | bytes 3145744 | tf_op jit(solution)/shard_map/all_gather | solution.py:26
  98.1 0.2 mul.34
  98.2 5.9 %fusion = f32[384,1024]{1,0:T(8,128)S(1)} fusion(f32[1,1,768,1024]{3,2,1,0:T(8,128)} %all-gather.15.cloned.1.call-done, f32[48,8,6,128]{3,2,1,0:T(8,128)S(1)} %bitcast.40, f32[384,1,1,768]{3,0,2,1:T(8,128)S(1)} %copy-done.1), kind=kOutput, calls=%fused_computation | convolution fusion | flops 3624173568 | bytes 7077888 | tf_op jit(solution)/shard_map/dot_general | solution.py:27
  104.2 16.9 %all-gather.9.cloned.1.call-done = f32[384,1,1,768]{3,0,2,1:T(8,128)} async-done(((f32[192,1,1,768]{3,0,2,1:T(8,128)}), f32[384,1,1,768]{3,0,2,1:T(8,128)}) %all-gather.9.cloned.1.call-update) | async-done | bytes 1179664 | tf_op jit(solution)/shard_map/all_gather | solution.py:20
  121.1 62.1 %all-gather.11.cloned.1.call-done = f32[1,1,768,1024]{3,2,1,0:T(8,128)} async-done(((f32[1,1,96,1024]{3,2,1,0:T(8,128)}), f32[1,1,768,1024]{3,2,1,0:T(8,128)}) %all-gather.11.cloned.1.call-update) | async-done | bytes 3145744 | tf_op jit(solution)/shard_map/all_gather | solution.py:26
  183.1 0.2 mul.31
  183.3 7.1 %fusion.4 = f32[384,1024]{1,0:T(8,128)} fusion(f32[384,1024]{1,0:T(8,128)S(1)} %fusion, f32[1,1,768,1024]{3,2,1,0:T(8,128)} %all-gather.11.cloned.1.call-done, f32[48,8,6,128]{3,2,1,0:T(8,128)S(1)} %bitcast.41, f32[384,1,1,768]{3,0,2,1:T(8,128)S(1)} %copy-done.2), kind=kOutput, calls=%fused_computation.5 | convolution fusion | flops 3624566784 | bytes 8650752 | tf_op jit(solution)/shard_map/dot_general | solution.py:27
  190.4 0.0 reduce-scatter.2.cloned.1.call-update
  190.5 0.7 copy-done.5
  191.1 0.2 broadcast_in_dim.2
  191.3 0.3 copy.25
  191.6 6.7 %reduce-scatter.2.cloned.1.call-done = f32[192,1024]{1,0:T(8,128)} async-done(((f32[384,1024]{1,0:T(8,128)}), f32[192,1024]{1,0:T(8,128)}) %reduce-scatter.2.cloned.1.call-update) | async-done | bytes 786448 | tf_op jit(solution)/shard_map/reduce_scatter | solution.py:40
  198.3 1.3 fusion.11
  199.6 33.9 %psum.7 = f32[1024]{0:T(1024)S(1)} all-reduce(f32[1024]{0:T(1024)S(1)} %fusion.11), channel_id=1, replica_groups=mesh['row'=8,'col'=2,'fiber'=2] {'row','fiber'}, use_global_device_ids=true, to_apply=%region_2.0 | all-reduce | flops 1024 | bytes 8192 | tf_op jit(solution)/shard_map/psum | solution.py:44
  233.5 0.0 copy-done
  233.5 1.0 broadcast_divide_fusion
  (12 shorter events, 0.0 us)
Async XLA Ops:
  6.5 3.7 %copy-start.3 = (f32[1,2,96,1024]{3,2,1,0:T(8,128)S(1)}, f32[1,2,96,1024]{3,2,1,0:T(8,128)}, u32[]{:S(2)}) copy-start(f32[1,2,96,1024]{3,2,1,0:T(8,128)} %param.5) | copy-start | bytes 2359300
  6.5 29.3 %all-gather.13.cloned.1.call-start = ((), (), s32[]{:S(2)}) async-start(), calls=%async_computation.4 | async-start | bytes 1769472 | tf_op jit(solution)/shard_map/all_gather | solution.py:20
  10.2 87.9 %all-gather.15.cloned.1.call-start = ((), (), s32[]{:S(2)}) async-start(), calls=%async_computation.5 | async-start | bytes 3538944 | tf_op jit(solution)/shard_map/all_gather | solution.py:26
  11.2 1.7 copy-start.4
  11.2 109.8 %all-gather.9.cloned.1.call-start = ((), (), s32[]{:S(2)}) async-start(), calls=%async_computation.2 | async-start | bytes 1769472 | tf_op jit(solution)/shard_map/all_gather | solution.py:20
  12.2 170.9 %all-gather.11.cloned.1.call-start = ((), (), s32[]{:S(2)}) async-start(), calls=%async_computation.3 | async-start | bytes 3538944 | tf_op jit(solution)/shard_map/all_gather | solution.py:26
  12.8 185.5 %reduce-scatter.2.cloned.1.call-start = ((), (), s32[]{:S(2)}) async-start(), calls=%async_computation.1 | async-start | bytes 2359296 | tf_op jit(solution)/shard_map/reduce_scatter | solution.py:40
  35.8 62.4 %copy-start.1 = (f32[384,1,1,768]{3,0,2,1:T(8,128)S(1)}, f32[384,1,1,768]{3,0,2,1:T(8,128)}, u32[]{:S(2)}) copy-start(f32[384,1,1,768]{3,0,2,1:T(8,128)} %all-gather.13.cloned.1.call-done) | copy-start | bytes 3538948
  121.1 62.3 %copy-start.2 = (f32[384,1,1,768]{3,0,2,1:T(8,128)S(1)}, f32[384,1,1,768]{3,0,2,1:T(8,128)}, u32[]{:S(2)}) copy-start(f32[384,1,1,768]{3,0,2,1:T(8,128)} %all-gather.9.cloned.1.call-done) | copy-start | bytes 3538948
  190.4 0.7 copy-start.5
  198.3 35.2 %copy-start = (f32[192,1024]{1,0:T(8,128)S(1)}, f32[192,1024]{1,0:T(8,128)}, u32[]{:S(2)}) copy-start(f32[192,1024]{1,0:T(8,128)} %reduce-scatter.2.cloned.1.call-done) | copy-start | bytes 2359300
Sparse Core Ops, SparseCore 0:
  10.3 25.4 all-gather.12
  38.0 60.0 all-gather.14
  99.6 21.4 all-gather.8
  123.1 60.0 all-gather.10
  190.6 7.6 reduce-scatter.1
where the time goes:
time: 241 us
  waiting for transfers between devices  171 us (71%)
  blocking collectives  33.9 us (14%)
  between operations  13.2 us (5%)
  matrix products  13 us (5%)
  local copies, waits for them, and re-layouts  6.99 us (3%)
    all_gather x2, waiting for transfers between devices, local(): lax.all_gather(b_panels[0, section_index], 'row', axis=0, tiled=True)  124 us
    all_gather x2, waiting for transfers between devices, local(): lax.all_gather(a_panels[:, 0, section_index, :], 'col', axis=0, tiled=True)  39.8 us
    psum x1, blocking collectives, local(): totals = lax.psum(jnp.sum(inflated, axis=0), ('row', 'fiber'))  33.9 us
    dot_general x2, matrix products, local(): jnp.dot(left_panel, right_panel, precision=lax.Precision.HIGHEST, preferr...  13 us
    reduce_scatter x1, waiting for transfers between devices, local(): lax.psum_scatter(running_sum, 'fiber', scatter_dimension=0, tiled=True)  6.67 us
  transfers between devices with their start and end apart: 5, of which 5 were waited for; matrix products, arithmetic and copies ran while one was open for 4% of the time, Pallas kernels for 0%

commit v1 on v0

--- a/solution.py
+++ b/solution.py
@@ -41,7 +41,7 @@
     keep_share = lax.dynamic_slice_in_dim(keep_full, layer_index * share_rows, share_rows, 0)
     product = merged * keep_share
     inflated = product * product
-    totals = lax.psum(jnp.sum(inflated, axis=0), ("row", "fiber"))
+    totals = jnp.sum(lax.all_gather(jnp.sum(inflated, axis=0), ("row", "fiber")), axis=0)
     row_count = share_rows * lax.axis_size("row") * fibers
     return inflated / (totals / row_count + EPS)
 

time: 241 us -> 229 us (0.950)
  blocking collectives: 33.9 us -> 21.9 us
    psum x1 -> x0, blocking collectives: 33.9 us -> none  [local(): totals = lax.psum(jnp.sum(inflated, axis=0), ('row', 'fiber'))]
    all_gather x0 -> x1, blocking collectives: none -> 21.9 us  [local(): lax.all_gather(jnp.sum(inflated, axis=0), ('row', 'fiber'))]
where the time goes in v1:
time: 229 us
  waiting for transfers between devices  171 us (75%)
  blocking collectives  21.9 us (10%)
  between operations  13.3 us (6%)
  matrix products  13 us (6%)
  local copies, waits for them, and re-layouts  7.01 us (3%)
  other arithmetic  2.38 us (1%)
    all_gather x2, waiting for transfers between devices, local(): lax.all_gather(b_panels[0, section_index], 'row', axis=0, tiled=True)  124 us
    all_gather x2, waiting for transfers between devices, local(): lax.all_gather(a_panels[:, 0, section_index, :], 'col', axis=0, tiled=True)  39.8 us
    all_gather x1, blocking collectives, local(): lax.all_gather(jnp.sum(inflated, axis=0), ('row', 'fiber'))  21.9 us
    dot_general x2, matrix products, local(): jnp.dot(left_panel, right_panel, precision=lax.Precision.HIGHEST, preferr...  13 us
    reduce_scatter x1, waiting for transfers between devices, local(): lax.psum_scatter(running_sum, 'fiber', scatter_dimension=0, tiled=True)  6.67 us
  transfers between devices with their start and end apart: 5, of which 5 were waited for; matrix products, arithmetic and copies ran while one was open for 4% of the time, Pallas kernels for 0%

profile of v1, /device:TPU:0, one launch (start us, length us, event | category | flops | bytes accessed | tf_op | source)
XLA Modules:
  0.0 229.1 jit_solution(15465286194301561984)
XLA Ops:
  6.5 0.0 all-gather.14.cloned.1.call-start
  6.5 2.8 %fusion.12 = (f32[192,1,1,768]{3,2,1,0:T(1,128)S(1)}, f32[192,1,1,768]{3,2,1,0:T(1,128)S(1)}) fusion(f32[192,1,2,768]{3,2,1,0:T(2,128)} %param.4), kind=kLoop, calls=%fused_computation.20 | loop fusion | bytes 2359296 | tf_op jit(solution)/shard_map/slice | solution.py:20
  9.3 0.9 copy.14
  10.2 0.0 all-gather.14.cloned.1.call-update
  10.2 0.0 all-gather.16.cloned.1.call-start
  10.2 0.0 copy-done.3
  10.2 0.9 fusion.13
  11.2 0.0 all-gather.16.cloned.1.call-update
  11.2 0.0 all-gather.10.cloned.1.call-start
  11.3 0.9 copy.13
  12.2 0.0 all-gather.10.cloned.1.call-update
  12.2 0.0 all-gather.12.cloned.1.call-start
  12.3 0.5 all-gather.12.cloned.1.call-update
  12.8 0.0 reduce-scatter.2.cloned.1.call-start
  12.8 0.0 copy-done.4
  12.9 23.0 %all-gather.14.cloned.1.call-done = f32[384,1,1,768]{3,0,2,1:T(8,128)} async-done(((f32[192,1,1,768]{3,0,2,1:T(8,128)}), f32[384,1,1,768]{3,0,2,1:T(8,128)}) %all-gather.14.cloned.1.call-update) | async-done | bytes 1179664 | tf_op jit(solution)/shard_map/all_gather | solution.py:20
  35.8 62.2 %all-gather.16.cloned.1.call-done = f32[1,1,768,1024]{3,2,1,0:T(8,128)} async-done(((f32[1,1,96,1024]{3,2,1,0:T(8,128)}), f32[1,1,768,1024]{3,2,1,0:T(8,128)}) %all-gather.16.cloned.1.call-update) | async-done | bytes 3145744 | tf_op jit(solution)/shard_map/all_gather | solution.py:26
  98.1 0.2 mul.34
  98.2 5.9 %fusion = f32[384,1024]{1,0:T(8,128)S(1)} fusion(f32[1,1,768,1024]{3,2,1,0:T(8,128)} %all-gather.16.cloned.1.call-done, f32[48,8,6,128]{3,2,1,0:T(8,128)S(1)} %bitcast.40, f32[384,1,1,768]{3,0,2,1:T(8,128)S(1)} %copy-done.1), kind=kOutput, calls=%fused_computation | convolution fusion | flops 3624173568 | bytes 7077888 | tf_op jit(solution)/shard_map/dot_general | solution.py:27
  104.2 16.9 %all-gather.10.cloned.1.call-done = f32[384,1,1,768]{3,0,2,1:T(8,128)} async-done(((f32[192,1,1,768]{3,0,2,1:T(8,128)}), f32[384,1,1,768]{3,0,2,1:T(8,128)}) %all-gather.10.cloned.1.call-update) | async-done | bytes 1179664 | tf_op jit(solution)/shard_map/all_gather | solution.py:20
  121.1 62.1 %all-gather.12.cloned.1.call-done = f32[1,1,768,1024]{3,2,1,0:T(8,128)} async-done(((f32[1,1,96,1024]{3,2,1,0:T(8,128)}), f32[1,1,768,1024]{3,2,1,0:T(8,128)}) %all-gather.12.cloned.1.call-update) | async-done | bytes 3145744 | tf_op jit(solution)/shard_map/all_gather | solution.py:26
  183.1 0.2 mul.31
  183.3 7.1 %fusion.4 = f32[384,1024]{1,0:T(8,128)} fusion(f32[384,1024]{1,0:T(8,128)S(1)} %fusion, f32[1,1,768,1024]{3,2,1,0:T(8,128)} %all-gather.12.cloned.1.call-done, f32[48,8,6,128]{3,2,1,0:T(8,128)S(1)} %bitcast.41, f32[384,1,1,768]{3,0,2,1:T(8,128)S(1)} %copy-done.2), kind=kOutput, calls=%fused_computation.5 | convolution fusion | flops 3624566784 | bytes 8650752 | tf_op jit(solution)/shard_map/dot_general | solution.py:27
  190.4 0.0 reduce-scatter.2.cloned.1.call-update
  190.5 0.7 copy-done.5
  191.1 0.2 broadcast_in_dim.2
  191.3 0.3 copy.29
  191.6 6.7 %reduce-scatter.2.cloned.1.call-done = f32[192,1024]{1,0:T(8,128)} async-done(((f32[384,1024]{1,0:T(8,128)}), f32[192,1024]{1,0:T(8,128)}) %reduce-scatter.2.cloned.1.call-update) | async-done | bytes 786448 | tf_op jit(solution)/shard_map/reduce_scatter | solution.py:40
  198.3 1.3 fusion.11
  199.6 21.9 %all-gather.4 = f32[16384]{0:T(1024)S(1)} all-gather(f32[1024]{0:T(1024)S(1)} %fusion.11), channel_id=6, replica_groups=mesh['row'=8,'col'=2,'fiber'=2] {'row','fiber'}, dimensions={0}, use_global_device_ids=true | all-gather | bytes 69632 | tf_op jit(solution)/shard_map/all_gather | solution.py:44
  221.6 0.0 copy-done
  221.6 1.0 broadcast_divide_fusion
  (14 shorter events, 0.1 us)
Async XLA Ops:
  6.5 3.7 %copy-start.3 = (f32[1,2,96,1024]{3,2,1,0:T(8,128)S(1)}, f32[1,2,96,1024]{3,2,1,0:T(8,128)}, u32[]{:S(2)}) copy-start(f32[1,2,96,1024]{3,2,1,0:T(8,128)} %param.5) | copy-start | bytes 2359300
  6.5 29.3 %all-gather.14.cloned.1.call-start = ((), (), s32[]{:S(2)}) async-start(), calls=%async_computation.4 | async-start | bytes 1769472 | tf_op jit(solution)/shard_map/all_gather | solution.py:20
  10.2 87.9 %all-gather.16.cloned.1.call-start = ((), (), s32[]{:S(2)}) async-start(), calls=%async_computation.5 | async-start | bytes 3538944 | tf_op jit(solution)/shard_map/all_gather | solution.py:26
  11.2 1.7 copy-start.4
  11.2 109.8 %all-gather.10.cloned.1.call-start = ((), (), s32[]{:S(2)}) async-start(), calls=%async_computation.2 | async-start | bytes 1769472 | tf_op jit(solution)/shard_map/all_gather | solution.py:20
  12.2 170.9 %all-gather.12.cloned.1.call-start = ((), (), s32[]{:S(2)}) async-start(), calls=%async_computation.3 | async-start | bytes 3538944 | tf_op jit(solution)/shard_map/all_gather | solution.py:26
  12.8 185.5 %reduce-scatter.2.cloned.1.call-start = ((), (), s32[]{:S(2)}) async-start(), calls=%async_computation.1 | async-start | bytes 2359296 | tf_op jit(solution)/shard_map/reduce_scatter | solution.py:40
  35.8 62.4 %copy-start.1 = (f32[384,1,1,768]{3,0,2,1:T(8,128)S(1)}, f32[384,1,1,768]{3,0,2,1:T(8,128)}, u32[]{:S(2)}) copy-start(f32[384,1,1,768]{3,0,2,1:T(8,128)} %all-gather.14.cloned.1.call-done) | copy-start | bytes 3538948
  121.1 62.3 %copy-start.2 = (f32[384,1,1,768]{3,0,2,1:T(8,128)S(1)}, f32[384,1,1,768]{3,0,2,1:T(8,128)}, u32[]{:S(2)}) copy-start(f32[384,1,1,768]{3,0,2,1:T(8,128)} %all-gather.10.cloned.1.call-done) | copy-start | bytes 3538948
  190.4 0.7 copy-start.5
  198.3 23.3 %copy-start = (f32[192,1024]{1,0:T(8,128)S(1)}, f32[192,1024]{1,0:T(8,128)}, u32[]{:S(2)}) copy-start(f32[192,1024]{1,0:T(8,128)} %reduce-scatter.2.cloned.1.call-done) | copy-start | bytes 2359300
Sparse Core Ops, SparseCore 0:
  10.3 25.4 all-gather.13
  38.0 60.0 all-gather.15
  99.6 21.4 all-gather.9
  123.1 60.0 all-gather.11
  190.6 7.6 reduce-scatter.1
